TPU v7x, 32 devices: a whole 2x2x4 slice. The times are simulated.
32 devices in a mesh: row: 4 (over y, x), col: 8 (over z, core).
Axes of the slice: x: 2, y: 2, z: 4, core: 2. Of those that a mesh axis runs over, the one named last changes fastest.
Arguments:
- fact_block: int32 [98304, 1], P(('row', 'col')), may hold values from 0 to 31; in each aligned block of 3072 rows (0 to 3071, 3072 to 6143, ...) at most 192 rows name the same one
- fact_offset: int32 [98304], P(('row', 'col')), may hold values from 0 to 2047
- fact_date: int32 [98304], P(('row', 'col')), may hold values from 0 to 2555
- revenue: bfloat16 [98304], P(('row', 'col')), may hold values from 0.5 to 4
- supplier_words: int32 [2208], P('col'), may hold values from 0 to 1073741823
- date_words: int32 [88], P('col'), may hold values from 0 to 1073741823
- candidates: int32 [1024], replicated, may hold values from 0 to 65535
Outputs:
- supplier_revenue: float32 [65536], P(('row', 'col'))
- candidate_revenue: float32 [1024], replicated
- candidate_total: float32 [], replicated
Inputs may be any that keep to these rules, and one draw needn't show every extreme that they name: `fact_block`: each device's rows name no owner block more than 192 times. `candidates`: ids may repeat.
All inputs are finite; a program needn't handle non-finite values.
Results may differ from a plain program's by a relative error of at most 0.0003.
Values sent between devices are 32-bit elements; how exact they have to be, the bound alone decides.
A program may use at most 64 MiB of HBM per device.

v0:
```python
import jax
import jax.numpy as jnp
from jax import lax
from jax.sharding import PartitionSpec as P

SUP_DEV = 2048


def filtered_revenue(owner, fact_offset, fact_date, revenue, supplier_all, date_all):
    words_per_block = (SUP_DEV + 29) // 30
    word_index = owner * words_per_block + fact_offset // 30
    supplier_word = jnp.take(supplier_all, word_index)
    supplier_bit = jnp.bitwise_and(jnp.right_shift(supplier_word, fact_offset % 30), 1)
    date_slot = fact_date // 30
    positions = jnp.arange(date_all.shape[0], dtype=jnp.int32)
    date_word = jnp.sum(
        jnp.where(date_slot[:, None] == positions[None, :], date_all[None, :], 0), axis=1
    )
    date_bit = jnp.bitwise_and(jnp.right_shift(date_word, fact_date % 30), 1)
    return jnp.where(supplier_bit * date_bit == 1, revenue, jnp.zeros_like(revenue))


def per_device(fact_block, fact_offset, fact_date, revenue, supplier_words, date_words, candidates):
    devices = lax.axis_size("row") * lax.axis_size("col")
    supplier_all, date_all = (
        lax.all_gather(supplier_words, "col", axis=0, tiled=True),
        lax.all_gather(date_words, "col", axis=0, tiled=True),
    )
    owner = fact_block[:, 0]
    masked = filtered_revenue(owner, fact_offset, fact_date, revenue, supplier_all, date_all)
    row_count = fact_offset.shape[0]
    capacity = max(2, 2 * row_count // devices)
    row_ids = jnp.arange(row_count, dtype=jnp.int32)
    earlier = (owner[:, None] == owner[None, :]) & (row_ids[None, :] < row_ids[:, None])
    ranking = jnp.sum(earlier, axis=1, dtype=jnp.int32)
    slot_index = owner * capacity + ranking
    slot_revenue = (
        jnp.zeros((devices * capacity,), jnp.float32).at[slot_index].set(masked.astype(jnp.float32))
    )
    slot_offset = (
        jnp.zeros((devices * capacity,), jnp.float32)
        .at[slot_index]
        .set(fact_offset.astype(jnp.float32))
    )
    payload = jnp.stack((slot_revenue, slot_offset), axis=-1)
    payload = payload.reshape(lax.axis_size("row"), lax.axis_size("col"), 2 * capacity)
    arrived = lax.all_to_all(
        lax.all_to_all(payload, "row", split_axis=0, concat_axis=0, tiled=True),
        "col",
        split_axis=1,
        concat_axis=1,
        tiled=True,
    )
    arrived = arrived.reshape(-1, 2)
    owned = jax.ops.segment_sum(
        arrived[:, 0], arrived[:, 1].astype(jnp.int32), num_segments=SUP_DEV
    )
    global_id = owner * SUP_DEV + fact_offset
    onehot_cands = (global_id[:, None] == candidates[None, :]).astype(jnp.bfloat16)
    own_terms = jnp.dot(masked[None, :], onehot_cands, preferred_element_type=jnp.float32)[0]
    candidate_revenue = lax.psum(own_terms, ("row", "col"))
    candidate_total = jnp.sum(candidate_revenue)
    return (owned, candidate_revenue, candidate_total)


def solution(mesh):
    in_specs = (
        P(("row", "col"), None),
        P(("row", "col")),
        P(("row", "col")),
        P(("row", "col")),
        P("col"),
        P("col"),
        P(),
    )
    out_specs = (P(("row", "col")), P(), P())
    return jax.shard_map(
        per_device, mesh=mesh, in_specs=in_specs, out_specs=out_specs, check_vma=False
    )
```

profile of v0, /device:TPU:20, one launch (start us, length us, event | category | flops | bytes accessed | tf_op | source)
XLA Modules:
  0.0 186.4 jit_solution(15897103582751986480)
XLA Ops:
  0.6 1.2 dynamic-slice
  3.2 3.9 %convert_reduce_fusion = s32[3072]{0:T(1024)S(1)} fusion(s32[3072]{0:T(1024)} %bitcast.11), kind=kLoop, calls=%fused_computation.4 | loop fusion | flops 47182848 | bytes 24576 | tf_op jit(solution)/shard_map/reduce_sum | solution.py:35
  7.0 0.7 compare_select_fusion
  7.8 0.7 add_select_fusion.1
  8.5 0.8 multiply_add_fusion
  9.3 0.9 dynamic-update-slice.1
  10.2 0.9 dynamic-update-slice
  11.0 21.6 %all-reduce.2 = (s32[88]{0:T(128)S(1)}, s32[2208]{0:T(1024)S(1)}) all-reduce(s32[88]{0:T(128)S(1)} %dynamic-update-slice.1, s32[2208]{0:T(1024)S(1)} %dynamic-update-slice), channel_id=1, replica_groups=mesh['row'=4,'col'=8] {'col'}, use_global_device_ids=true, to_apply=%add.1 | all-reduce | flops 2296 | bytes 18368
  32.6 0.3 select_reduce_fusion
  32.9 0.0 copy-start
  32.9 0.0 copy-start.1
  32.9 0.0 copy-start.2
  32.9 0.0 copy-start.4
  32.9 17.4 %gather_fusion = s32[3072]{0:T(1024)S(1)} fusion(s32[2208]{0:T(1024)S(1)} %get-tuple-element.4, s32[3072]{0:T(1024)S(1)} %get-tuple-element.8), kind=kCustom, calls=%fused_computation | custom fusion | bytes 36864 | tf_op jit(solution)/shard_map/jit(_take)/gather | solution.py:12
  50.3 0.0 copy-done
  50.4 0.0 copy-done.1
  50.4 0.0 copy-done.2
  50.4 0.0 copy-done.4
  50.4 11.8 %scatter_custom_fusion = f32[6144]{0:T(1024)S(1)} fusion(s32[3072]{0:T(1024)S(1)} %bitcast.16, f32[3072]{0:T(1024)S(1)} %get-tuple-element.5, f32[]{:T(128)} %constant.30.clone.1), kind=kCustom, calls=%fused_computation.35 | custom fusion | bytes 24580 | tf_op jit(solution)/shard_map/scatter | solution.py:38
  62.2 11.8 %scatter_custom_fusion.1 = f32[6144]{0:T(1024)S(1)} fusion(s32[3072]{0:T(1024)S(1)} %bitcast.17, f32[3072]{0:T(1024)S(1)} %get-tuple-element.9, f32[]{:T(128)} %constant.30.clone.1), kind=kCustom, calls=%fused_computation.33 | custom fusion | bytes 24580 | tf_op jit(solution)/shard_map/scatter | solution.py:43
  74.1 0.0 copy-start.5
  74.1 1.1 copy.14
  75.2 2.7 %reshape.27 = f32[4,8,384]{2,1,0:T(8,128)} reshape(f32[6144,2]{1,0:T(8,128)S(1)} %copy.14) | data formatting | bytes 98304 | tf_op jit(solution)/shard_map/reshape | solution.py:46
  77.9 4.2 %all-to-all-start = ((f32[4,8,384]{2,1,0:T(8,128)}), f32[4,8,384]{2,1,0:T(8,128)S(1)}, u32[]{:S(2)}, u32[]{:S(2)}) async-start(f32[4,8,384]{2,1,0:T(8,128)} %reshape.27), calls=%async_computation | async-start | bytes 98304 | tf_op jit(solution)/shard_map/all_to_all | solution.py:48
  82.2 3.5 %all-to-all-done = f32[4,8,384]{2,1,0:T(8,128)S(1)} async-done(((f32[4,8,384]{2,1,0:T(8,128)}), f32[4,8,384]{2,1,0:T(8,128)S(1)}, u32[]{:S(2)}, u32[]{:S(2)}) %all-to-all-start) | async-done | bytes 49184 | tf_op jit(solution)/shard_map/all_to_all | solution.py:48
  85.7 0.6 copy.15
  86.3 10.8 %all-to-all-start.1 = ((f32[4,8,384]{2,0,1:T(4,128)}), f32[4,8,384]{2,0,1:T(4,128)S(1)}, u32[]{:S(2)}, u32[]{:S(2)}) async-start(f32[4,8,384]{2,0,1:T(4,128)} %copy.15), calls=%async_computation.1 | async-start | bytes 98304 | tf_op jit(solution)/shard_map/all_to_all | solution.py:47
  97.1 0.0 copy-done.5
  97.1 2.0 %fusion.1 = f32[1,1024]{1,0:T(1,128)S(1)} fusion(bf16[3072,1]{0,1:T(2,128)(2,1)S(1)} %reshape.72, s32[1024]{0:T(1024)S(1)} %copy-done.5, s32[3072]{0:T(1024)S(1)} %get-tuple-element.7), kind=kOutput, calls=%fused_computation.7 | convolution fusion | flops 9437184 | bytes 26624 | tf_op jit(solution)/shard_map/dot_general | solution.py:60
  99.1 40.9 %psum.7 = f32[1024]{0:T(1024)S(1)} all-reduce(f32[1024]{0:T(1024)S(1)} %bitcast.19), channel_id=1, replica_groups=mesh['row'=4,'col'=8] {'row','col'}, use_global_device_ids=true, to_apply=%region_5.6 | all-reduce | flops 1024 | bytes 8192 | tf_op jit(solution)/shard_map/psum | solution.py:61
  140.0 0.0 copy-start.3
  140.0 0.6 reduce_sum.32
  140.6 0.0 all-to-all-done.1
  140.6 3.2 %reshape.28 = f32[6144,2]{1,0:T(8,128)S(1)} reshape(f32[4,8,384]{2,1,0:T(8,128)S(1)} %copy.16) | data formatting | bytes 98304 | tf_op jit(solution)/shard_map/reshape | solution.py:54
  143.7 0.9 slice_reduce_fusion
  144.6 0.0 copy-done.3
  144.6 1.7 fusion.5
  146.3 40.0 %scatter_custom_fusion.2 = f32[2048]{0:T(1024)} fusion(s32[6144]{0:T(1024)S(1)} %fusion.5, f32[6144]{0:T(1024)S(1)} %slice_reduce_fusion, f32[]{:T(128)} %constant.30.clone.1), kind=kCustom, calls=%fused_computation.43 | custom fusion | flops 6144 | bytes 8196 | tf_op jit(solution)/shard_map/scatter-add | solution.py:55
  (6 shorter events, 0.1 us)
Async XLA Ops:
  32.9 17.5 %copy-start = (s32[3072,1]{0,1:T(1,128)S(1)}, s32[3072,1]{0,1:T(1,128)}, u32[]{:S(2)}) copy-start(s32[3072,1]{0,1:T(1,128)} %param.7) | copy-start | bytes 36868
  32.9 17.5 %copy-start.1 = (s32[3072]{0:T(1024)S(1)}, s32[3072]{0:T(1024)}, u32[]{:S(2)}) copy-start(s32[3072]{0:T(1024)} %param.9) | copy-start | bytes 36868
  32.9 17.5 %copy-start.2 = (s32[3072]{0:T(1024)S(1)}, s32[3072]{0:T(1024)}, u32[]{:S(2)}) copy-start(s32[3072]{0:T(1024)} %param.8) | copy-start | bytes 36868
  32.9 17.5 %copy-start.4 = (bf16[3072]{0:T(1024)(128)(2,1)S(1)}, bf16[3072]{0:T(1024)(128)(2,1)}, u32[]{:S(2)}) copy-start(bf16[3072]{0:T(1024)(128)(2,1)} %param.10) | copy-start | bytes 18436
  74.1 23.0 %copy-start.5 = (s32[1024]{0:T(1024)S(1)}, s32[1024]{0:T(1024)}, u32[]{:S(2)}) copy-start(s32[1024]{0:T(1024)} %param.13) | copy-start | bytes 12292
  77.9 7.7 %all-to-all-start = ((f32[4,8,384]{2,1,0:T(8,128)}), f32[4,8,384]{2,1,0:T(8,128)S(1)}, u32[]{:S(2)}, u32[]{:S(2)}) async-start(f32[4,8,384]{2,1,0:T(8,128)} %reshape.27), calls=%async_computation | async-start | bytes 98304 | tf_op jit(solution)/shard_map/all_to_all | solution.py:48
  86.3 54.3 %all-to-all-start.1 = ((f32[4,8,384]{2,0,1:T(4,128)}), f32[4,8,384]{2,0,1:T(4,128)S(1)}, u32[]{:S(2)}, u32[]{:S(2)}) async-start(f32[4,8,384]{2,0,1:T(4,128)} %copy.15), calls=%async_computation.1 | async-start | bytes 98304 | tf_op jit(solution)/shard_map/all_to_all | solution.py:47
  140.0 4.7 %copy-start.3 = (f32[1024]{0:T(1024)}, f32[1024]{0:T(1024)S(1)}, u32[]{:S(2)}) copy-start(f32[1024]{0:T(1024)S(1)} %psum.7) | copy-start | bytes 12292
where the time goes:
time: 187 us; the launch traced here: 186 us
  blocking collectives  62.5 us (33%)
  local copies, waits for them, and re-layouts  52.5 us (28%)
  other arithmetic  48.8 us (26%)
  starting transfers between devices  15 us (8%)
  waiting for transfers between devices  3.5 us (2%)
  between operations  2.1 us (1%)
  matrix products  2 us (1%)
    psum x1, blocking collectives, per_device(): candidate_revenue = lax.psum(own_terms, ('row', 'col'))  40.9 us
    scatter-add x1, other arithmetic, per_device(): jax.ops.segment_sum(arrived[:, 0], arrived[:, 1].astype(jnp.int32), num_s...  40 us
    unnamed x1, blocking collectives  21.6 us
    gather x1, local copies, waits for them, and re-layouts, filtered_revenue(): supplier_word = jnp.take(supplier_all, word_index)  17.4 us
    scatter x1, local copies, waits for them, and re-layouts, per_device(): slot_offset = jnp.zeros((devices * capacity,), jnp.float32).at[slot_index...  11.8 us
    scatter x1, local copies, waits for them, and re-layouts, per_device(): jnp.zeros((devices * capacity,), jnp.float32).at[slot_index]  11.8 us
    all_to_all x1, starting transfers between devices, per_device(): lax.all_to_all(lax.all_to_all(payload, 'row', split_axis=0, concat_axis=0...  10.8 us
    all_to_all x1, starting transfers between devices, per_device(): lax.all_to_all(payload, 'row', split_axis=0, concat_axis=0, tiled=True)  4.22 us
  transfers between devices with their start and end apart: 2, of which 1 were waited for; matrix products, arithmetic and copies ran while one was open for 1% of the time, Pallas kernels for 0%

commit v1 on v0

--- a/solution.py
+++ b/solution.py
@@ -58,7 +58,7 @@
     global_id = owner * SUP_DEV + fact_offset
     onehot_cands = (global_id[:, None] == candidates[None, :]).astype(jnp.bfloat16)
     own_terms = jnp.dot(masked[None, :], onehot_cands, preferred_element_type=jnp.float32)[0]
-    candidate_revenue = lax.psum(own_terms, ("row", "col"))
+    candidate_revenue = lax.psum(lax.psum(own_terms, "col"), "row")
     candidate_total = jnp.sum(candidate_revenue)
     return (owned, candidate_revenue, candidate_total)
 

time: 187 us -> 172 us (0.920)
  the two profiles are of different devices: /device:TPU:20 before, /device:TPU:4 now
where the time goes in v1:
time: 172 us; the launch traced here: 171 us
  blocking collectives  54.8 us (32%)
  local copies, waits for them, and re-layouts  52.5 us (31%)
  other arithmetic  48.2 us (28%)
  starting transfers between devices  7.56 us (4%)
  waiting for transfers between devices  3.46 us (2%)
  between operations  2.12 us (1%)
  matrix products  2.01 us (1%)
    scatter-add x1, other arithmetic, per_device(): jax.ops.segment_sum(arrived[:, 0], arrived[:, 1].astype(jnp.int32), num_s...  39.4 us
    unnamed x1, blocking collectives  28.8 us
    psum x2, blocking collectives, per_device(): candidate_revenue = lax.psum(lax.psum(own_terms, 'col'), 'row')  26 us
    gather x1, local copies, waits for them, and re-layouts, filtered_revenue(): supplier_word = jnp.take(supplier_all, word_index)  17.4 us
    scatter x1, local copies, waits for them, and re-layouts, per_device(): jnp.zeros((devices * capacity,), jnp.float32).at[slot_index]  11.8 us
    scatter x1, local copies, waits for them, and re-layouts, per_device(): slot_offset = jnp.zeros((devices * capacity,), jnp.float32).at[slot_index...  11.8 us
    all_to_all x1, starting transfers between devices, per_device(): lax.all_to_all(payload, 'row', split_axis=0, concat_axis=0, tiled=True)  4.22 us
    reduce_sum x1, other arithmetic, per_device(): ranking = jnp.sum(earlier, axis=1, dtype=jnp.int32)  3.86 us
  transfers between devices with their start and end apart: 2, of which 1 were waited for; matrix products, arithmetic and copies ran while one was open for 2% of the time, Pallas kernels for 0%

profile of v1, /device:TPU:4, one launch (start us, length us, event | category | flops | bytes accessed | tf_op | source)
XLA Modules:
  0.0 170.6 jit_solution(9906170093563342530)
XLA Ops:
  0.6 1.2 dynamic-slice
  3.2 3.9 %convert_reduce_fusion = s32[3072]{0:T(1024)S(1)} fusion(s32[3072]{0:T(1024)} %bitcast.11), kind=kLoop, calls=%fused_computation.4 | loop fusion | flops 47182848 | bytes 24576 | tf_op jit(solution)/shard_map/reduce_sum | solution.py:35
  7.0 0.7 compare_select_fusion
  7.8 0.7 add_select_fusion.1
  8.5 0.8 multiply_add_fusion
  9.3 0.9 dynamic-update-slice.1
  10.2 0.9 dynamic-update-slice
  11.0 28.8 %all-reduce.2 = (s32[88]{0:T(128)S(1)}, s32[2208]{0:T(1024)S(1)}) all-reduce(s32[88]{0:T(128)S(1)} %dynamic-update-slice.1, s32[2208]{0:T(1024)S(1)} %dynamic-update-slice), channel_id=1, replica_groups=mesh['row'=4,'col'=8] {'col'}, use_global_device_ids=true, to_apply=%add.1 | all-reduce | flops 2296 | bytes 18368
  39.8 0.3 select_reduce_fusion
  40.1 0.0 copy-start
  40.1 0.0 copy-start.1
  40.1 0.0 copy-start.2
  40.1 0.0 copy-start.4
  40.1 17.4 %gather_fusion = s32[3072]{0:T(1024)S(1)} fusion(s32[2208]{0:T(1024)S(1)} %get-tuple-element.4, s32[3072]{0:T(1024)S(1)} %get-tuple-element.8), kind=kCustom, calls=%fused_computation | custom fusion | bytes 36864 | tf_op jit(solution)/shard_map/jit(_take)/gather | solution.py:12
  57.6 0.0 copy-done
  57.6 0.0 copy-done.1
  57.6 0.0 copy-done.2
  57.6 0.0 copy-done.4
  57.6 11.8 %scatter_custom_fusion = f32[6144]{0:T(1024)S(1)} fusion(s32[3072]{0:T(1024)S(1)} %bitcast.16, f32[3072]{0:T(1024)S(1)} %get-tuple-element.5, f32[]{:T(128)} %constant.30.clone.1), kind=kCustom, calls=%fused_computation.35 | custom fusion | bytes 24580 | tf_op jit(solution)/shard_map/scatter | solution.py:38
  69.5 11.8 %scatter_custom_fusion.1 = f32[6144]{0:T(1024)S(1)} fusion(s32[3072]{0:T(1024)S(1)} %bitcast.17, f32[3072]{0:T(1024)S(1)} %get-tuple-element.9, f32[]{:T(128)} %constant.30.clone.1), kind=kCustom, calls=%fused_computation.33 | custom fusion | bytes 24580 | tf_op jit(solution)/shard_map/scatter | solution.py:43
  81.3 0.0 copy-start.5
  81.3 1.1 copy.14
  82.4 2.7 %reshape.27 = f32[4,8,384]{2,1,0:T(8,128)} reshape(f32[6144,2]{1,0:T(8,128)S(1)} %copy.14) | data formatting | bytes 98304 | tf_op jit(solution)/shard_map/reshape | solution.py:46
  85.1 4.2 %all-to-all-start = ((f32[4,8,384]{2,1,0:T(8,128)}), f32[4,8,384]{2,1,0:T(8,128)S(1)}, u32[]{:S(2)}, u32[]{:S(2)}) async-start(f32[4,8,384]{2,1,0:T(8,128)} %reshape.27), calls=%async_computation | async-start | bytes 98304 | tf_op jit(solution)/shard_map/all_to_all | solution.py:48
  89.4 3.5 %all-to-all-done = f32[4,8,384]{2,1,0:T(8,128)S(1)} async-done(((f32[4,8,384]{2,1,0:T(8,128)}), f32[4,8,384]{2,1,0:T(8,128)S(1)}, u32[]{:S(2)}, u32[]{:S(2)}) %all-to-all-start) | async-done | bytes 49184 | tf_op jit(solution)/shard_map/all_to_all | solution.py:48
  92.8 0.6 copy.15
  93.5 3.3 %all-to-all-start.1 = ((f32[4,8,384]{2,0,1:T(4,128)}), f32[4,8,384]{2,0,1:T(4,128)S(1)}, u32[]{:S(2)}, u32[]{:S(2)}) async-start(f32[4,8,384]{2,0,1:T(4,128)} %copy.15), calls=%async_computation.1 | async-start | bytes 98304 | tf_op jit(solution)/shard_map/all_to_all | solution.py:47
  96.8 0.0 copy-done.5
  96.8 2.0 %fusion.1 = f32[1,1024]{1,0:T(1,128)S(1)} fusion(bf16[3072,1]{0,1:T(2,128)(2,1)S(1)} %reshape.72, s32[1024]{0:T(1024)S(1)} %copy-done.5, s32[3072]{0:T(1024)S(1)} %get-tuple-element.7), kind=kOutput, calls=%fused_computation.7 | convolution fusion | flops 9437184 | bytes 26624 | tf_op jit(solution)/shard_map/dot_general | solution.py:60
  98.8 17.0 %psum.14 = f32[1024]{0:T(1024)S(1)} all-reduce(f32[1024]{0:T(1024)S(1)} %bitcast.19), channel_id=1, replica_groups=mesh['row'=4,'col'=8] {'col'}, use_global_device_ids=true, to_apply=%region_5.6 | all-reduce | flops 1024 | bytes 8192 | tf_op jit(solution)/shard_map/psum | solution.py:61
  115.9 8.9 %psum.15 = f32[1024]{0:T(1024)S(1)} all-reduce(f32[1024]{0:T(1024)S(1)} %psum.14), channel_id=1, replica_groups=mesh['row'=4,'col'=8] {'row'}, use_global_device_ids=true, to_apply=%region_6.7 | all-reduce | flops 1024 | bytes 8192 | tf_op jit(solution)/shard_map/psum | solution.py:61
  124.8 0.0 copy-start.3
  124.8 0.6 reduce_sum.32
  125.4 0.0 all-to-all-done.1
  125.4 3.2 %reshape.28 = f32[6144,2]{1,0:T(8,128)S(1)} reshape(f32[4,8,384]{2,1,0:T(8,128)S(1)} %copy.16) | data formatting | bytes 98304 | tf_op jit(solution)/shard_map/reshape | solution.py:54
  128.6 0.9 slice_reduce_fusion
  129.5 0.0 copy-done.3
  129.5 1.7 %fusion.5 = s32[6144]{0:T(1024)S(1)} fusion(f32[6144,2]{1,0:T(8,128)S(1)} %reshape.28), kind=kLoop, calls=%fused_computation.13 | loop fusion | flops 6144 | bytes 49152 | tf_op jit(solution)/shard_map/convert_element_type | solution.py:56
  131.2 39.4 %scatter_custom_fusion.2 = f32[2048]{0:T(1024)} fusion(s32[6144]{0:T(1024)S(1)} %fusion.5, f32[6144]{0:T(1024)S(1)} %slice_reduce_fusion, f32[]{:T(128)} %constant.30.clone.1), kind=kCustom, calls=%fused_computation.43 | custom fusion | flops 6144 | bytes 8196 | tf_op jit(solution)/shard_map/scatter-add | solution.py:55
  (6 shorter events, 0.1 us)
Async XLA Ops:
  40.1 17.5 %copy-start = (s32[3072,1]{0,1:T(1,128)S(1)}, s32[3072,1]{0,1:T(1,128)}, u32[]{:S(2)}) copy-start(s32[3072,1]{0,1:T(1,128)} %param.7) | copy-start | bytes 36868
  40.1 17.5 %copy-start.1 = (s32[3072]{0:T(1024)S(1)}, s32[3072]{0:T(1024)}, u32[]{:S(2)}) copy-start(s32[3072]{0:T(1024)} %param.9) | copy-start | bytes 36868
  40.1 17.5 %copy-start.2 = (s32[3072]{0:T(1024)S(1)}, s32[3072]{0:T(1024)}, u32[]{:S(2)}) copy-start(s32[3072]{0:T(1024)} %param.8) | copy-start | bytes 36868
  40.1 17.5 %copy-start.4 = (bf16[3072]{0:T(1024)(128)(2,1)S(1)}, bf16[3072]{0:T(1024)(128)(2,1)}, u32[]{:S(2)}) copy-start(bf16[3072]{0:T(1024)(128)(2,1)} %param.10) | copy-start | bytes 18436
  81.3 15.5 %copy-start.5 = (s32[1024]{0:T(1024)S(1)}, s32[1024]{0:T(1024)}, u32[]{:S(2)}) copy-start(s32[1024]{0:T(1024)} %param.13) | copy-start | bytes 12292
  85.1 7.7 %all-to-all-start = ((f32[4,8,384]{2,1,0:T(8,128)}), f32[4,8,384]{2,1,0:T(8,128)S(1)}, u32[]{:S(2)}, u32[]{:S(2)}) async-start(f32[4,8,384]{2,1,0:T(8,128)} %reshape.27), calls=%async_computation | async-start | bytes 98304 | tf_op jit(solution)/shard_map/all_to_all | solution.py:48
  93.5 31.9 %all-to-all-start.1 = ((f32[4,8,384]{2,0,1:T(4,128)}), f32[4,8,384]{2,0,1:T(4,128)S(1)}, u32[]{:S(2)}, u32[]{:S(2)}) async-start(f32[4,8,384]{2,0,1:T(4,128)} %copy.15), calls=%async_computation.1 | async-start | bytes 98304 | tf_op jit(solution)/shard_map/all_to_all | solution.py:47
  124.8 4.7 %copy-start.3 = (f32[1024]{0:T(1024)}, f32[1024]{0:T(1024)S(1)}, u32[]{:S(2)}) copy-start(f32[1024]{0:T(1024)S(1)} %psum.15) | copy-start | bytes 12292
